TPU v7x, 512 devices: a whole 4x8x8 slice. The times are simulated.
512 devices in a mesh: grp: 16 (over y, core), ops: 32 (over x, z).
Axes of the slice: x: 4, y: 8, z: 8, core: 2. Of those that a mesh axis runs over, the one named last changes fastest.
Arguments:
- op_embed: bfloat16 [131072, 256], P(('grp', 'ops')), may hold values from -6 to 6
- machine_embed: bfloat16 [8192, 256], P('grp'), may hold values from -6 to 6
- cotangent: bfloat16 [131072, 256], P(('grp', 'ops')), may hold values from -6 to 6
- w_query: bfloat16 [256, 256], replicated, may hold values from -0.375 to 0.375
- w_key: bfloat16 [256, 256], replicated, may hold values from -0.375 to 0.375
- w_value: bfloat16 [256, 256], replicated, may hold values from -0.375 to 0.375
- slot_local: int32 [512, 16], P(('grp', 'ops')), may hold values from 0 to 3
- counts: int32 [131072, 16], P(('grp', 'ops')), may hold values from 0 to 128, as said below
Outputs:
- op_grad: bfloat16 [131072, 256], P(('grp', 'ops'))
- machine_grad: float32 [8192, 256], P(('grp', 'ops'))
- grad_wq: float32 [256, 256], replicated
- grad_wk: float32 [256, 256], replicated
- grad_wv: float32 [256, 256], replicated
Inputs may be any that keep to these rules, and one draw needn't show every extreme that they name: The eligible machines of slot e's block for operation o are its first counts[o, e] machines; 0 means the operation has no eligible machine in that block.
All inputs are finite; a program needn't handle non-finite values.
Results may differ from a plain program's by a relative error of at most 0.0056.
Values may be sent and summed in bfloat16 or wider, within the bound.
No kernel may reach another device: no remote copies, remote signals or barrier semaphores. Data moves between devices by JAX's collectives and lax.ppermute only.
A program may use at most 64 MiB of HBM per device.

v0:
```python
import jax
import jax.numpy as jnp
from jax import lax
from jax.sharding import PartitionSpec as P

HEADS = 8
BLK = 128
mean_scale = 0.08838834764831845


def slot_grads(queries, cotangent4, key_rows, value_rows, lengths):
    head_size = queries.shape[2]
    inv_root = head_size ** (-0.5)
    scores = (
        jnp.einsum("ohc,mhc->ohm", queries, key_rows, preferred_element_type=jnp.float32) * inv_root
    )
    sigmoid_score = jax.nn.sigmoid(scores)
    columns = lax.broadcasted_iota(jnp.int32, scores.shape, 2)
    eligible = columns < lengths[:, None, None]
    gates = jnp.where(eligible, sigmoid_score, 0.0).astype(jnp.bfloat16)
    value_dot = jnp.einsum(
        "ohc,mhc->ohm", cotangent4, value_rows, preferred_element_type=jnp.float32
    )
    dscore = jnp.where(
        eligible, mean_scale * value_dot * sigmoid_score * (1.0 - sigmoid_score) * inv_root, 0.0
    ).astype(jnp.bfloat16)
    query_part = jnp.einsum("ohm,mhc->ohc", dscore, key_rows, preferred_element_type=jnp.float32)
    key_grad = jnp.einsum(
        "ohm,ohc->mhc", dscore, queries, preferred_element_type=jnp.float32
    ).astype(jnp.bfloat16)
    value_grad = (
        mean_scale
        * jnp.einsum("ohm,ohc->mhc", gates, cotangent4, preferred_element_type=jnp.float32)
    ).astype(jnp.bfloat16)
    return (query_part, key_grad, value_grad)


def per_device(op_embed, machine_embed, cotangent, w_query, w_key, w_value, slot_local, counts):
    groups = lax.axis_size("grp")
    ops_count = op_embed.shape[0]
    model_width = op_embed.shape[1]
    head_size = model_width // HEADS
    machine_rows = machine_embed.shape[0]
    blocks_here = machine_rows // BLK
    highest = lax.Precision.HIGHEST
    both_weights = jnp.concatenate([w_key, w_value], axis=1)
    queries = jnp.dot(op_embed, w_query, preferred_element_type=jnp.float32).astype(jnp.bfloat16)
    wanted = lax.all_to_all(
        slot_local.reshape(groups, 1), "grp", split_axis=0, concat_axis=0, tiled=True
    )
    wanted_ids = wanted[:, 0]
    picker = wanted_ids[:, None] == jnp.arange(blocks_here, dtype=jnp.int32)[None, :]
    local_pairs = jnp.dot(machine_embed, both_weights, preferred_element_type=jnp.float32).astype(
        jnp.bfloat16
    )
    outgoing = local_pairs.reshape(blocks_here, BLK, 2 * model_width)[wanted_ids]
    fetched = lax.all_to_all(outgoing, "grp", split_axis=0, concat_axis=0, tiled=True)
    key_slots = fetched[:, :, :model_width].reshape(groups, BLK, HEADS, head_size)
    value_slots = fetched[:, :, model_width:].reshape(groups, BLK, HEADS, head_size)
    query_heads = queries.reshape(ops_count, HEADS, head_size)
    cot_heads = cotangent.reshape(ops_count, HEADS, head_size)

    def per_slot(summed_q, pieces):
        key_rows, value_rows, lengths = pieces
        query_part, key_grad, value_grad = slot_grads(
            query_heads, cot_heads, key_rows, value_rows, lengths
        )
        return (
            summed_q + query_part,
            (key_grad.reshape(BLK, model_width), value_grad.reshape(BLK, model_width)),
        )

    start_q = jnp.zeros((ops_count, HEADS, head_size), jnp.float32)
    summed_q, (key_grads, value_grads) = lax.scan(
        per_slot, start_q, (key_slots, value_slots, counts.T)
    )
    grad_query = summed_q.astype(jnp.bfloat16).reshape(ops_count, model_width)
    op_grad = (
        cotangent.astype(jnp.float32)
        + jnp.dot(grad_query, w_query.T, preferred_element_type=jnp.float32)
    ).astype(jnp.bfloat16)
    wq_term = jnp.einsum("od,oe->de", op_embed, grad_query, preferred_element_type=jnp.float32)
    returned = lax.all_to_all(
        jnp.concatenate([key_grads, value_grads], axis=2),
        "grp",
        split_axis=0,
        concat_axis=0,
        tiled=True,
    )
    summed = jnp.einsum(
        "gb,gr->br",
        picker.astype(jnp.bfloat16),
        returned.reshape(groups, BLK * 2 * model_width),
        preferred_element_type=jnp.float32,
    )
    summed = summed.reshape(machine_rows, 2 * model_width)
    key_total = summed[:, :model_width]
    value_total = summed[:, model_width:]
    machine_part = jnp.dot(key_total, w_key.astype(jnp.float32).T, precision=highest) + jnp.dot(
        value_total, w_value.astype(jnp.float32).T, precision=highest
    )
    embed_f = machine_embed.astype(jnp.float32)
    wk_term = jnp.dot(embed_f.T, key_total, precision=highest)
    wv_term = jnp.dot(embed_f.T, value_total, precision=highest)
    summed_total = lax.psum(machine_part, "ops")
    share_rows = machine_rows // lax.axis_size("ops")
    first_row = lax.axis_index("ops") * share_rows
    machine_grad = lax.dynamic_slice_in_dim(summed_total, first_row, share_rows, 0)
    weight_sums = lax.psum((wq_term, wk_term, wv_term), ("grp", "ops"))
    shard_count = float(groups * lax.axis_size("ops"))
    grad_wq = weight_sums[0] / shard_count
    grad_wk = weight_sums[1] / shard_count
    grad_wv = weight_sums[2] / shard_count
    return (op_grad, machine_grad, grad_wq, grad_wk, grad_wv)


def solution(mesh):
    return jax.shard_map(
        per_device,
        mesh=mesh,
        in_specs=(
            P(("grp", "ops"), None),
            P("grp", None),
            P(("grp", "ops"), None),
            P(),
            P(),
            P(),
            P(("grp", "ops"), None),
            P(("grp", "ops"), None),
        ),
        out_specs=(P(("grp", "ops"), None), P(("grp", "ops"), None), P(), P(), P()),
        check_vma=False,
    )
```

profile of v0, /device:TPU:8, one launch (start us, length us, event | category | flops | bytes accessed | tf_op | source)
XLA Modules:
  0.0 657.2 jit_solution(9235457132968034616)
XLA Ops:
  7.2 1.4 copy.46
  8.6 9.1 %all-to-all-start = ((s32[16,1,1]{2,1,0:T(1,128)}), s32[16,1,1]{2,1,0:T(1,128)S(1)}, u32[]{:S(2)}, u32[]{:S(2)}) async-start(s32[16,1,1]{2,1,0:T(1,128)} %copy.46), calls=%async_computation | async-start | bytes 16384 | tf_op jit(solution)/shard_map/all_to_all | solution.py:48
  18.9 4.9 all-to-all-done
  24.2 2.0 gather_fusion
  26.2 5.1 all-to-all-start.1
  31.7 46.8 %all-to-all-done.1 = bf16[16,128,512]{2,1,0:T(8,128)(2,1)S(1)} async-done(((bf16[16,128,512]{2,1,0:T(8,128)(2,1)}), bf16[16,128,512]{2,1,0:T(8,128)(2,1)S(1)}, u32[]{:S(2)}, u32[]{:S(2)}) %all-to-all-start.1) | async-done | bytes 2097184 | tf_op jit(solution)/shard_map/all_to_all | solution.py:57
  78.6 1.6 fusion.38
  80.2 1.7 copy.47
  81.9 1.3 copy.48
  83.2 63.6 %while.15 = (s32[]{:T(128)}, f32[256,8,32]{0,2,1:T(8,128)S(1)}, bf16[16,128,256]{1,2,0:T(8,128)(2,1)}, bf16[16,128,256]{1,2,0:T(8,128)(2,1)}, bf16[16,128,8,32]{...) while((s32[]{:T(128)}, f32[256,8,32]{0,2,1:T(8,128)S(1)}, ...), condition=%wide.region_1.2_spmd.clone, body=%wide.region_0.1_spmd.clone.sunk | while | flops 87785472 | bytes 6361235 | solution.py:74
  84.4 1.3 fusion.80
  88.4 1.3 fusion.80
  92.4 1.3 fusion.80
  96.3 1.3 fusion.80
  100.3 1.3 fusion.80
  104.3 1.3 fusion.80
  108.2 1.3 fusion.80
  112.2 1.3 fusion.80
  116.2 1.3 fusion.80
  120.2 1.3 fusion.80
  124.1 1.3 fusion.80
  128.1 1.3 fusion.80
  132.1 1.3 fusion.80
  140.1 1.3 fusion.80
  144.0 1.3 fusion.80
  146.8 3.1 pad_maximum_fusion
  149.9 6.9 %all-to-all-start.2 = ((bf16[16,128,512]{1,2,0:T(8,128)(2,1)}), bf16[16,128,512]{1,2,0:T(8,128)(2,1)}, u32[]{:S(2)}, u32[]{:S(2)}) async-start(bf16[16,128,512]{1,2,0:T(8,128)(2,1)} %pad_maximum_fusion), calls=%async_computation.2 | async-start | bytes 4194304 | tf_op jit(solution)/shard_map/all_to_all | solution.py:83
  157.7 46.3 %all-to-all-done.2 = bf16[16,128,512]{1,2,0:T(8,128)(2,1)} async-done(((bf16[16,128,512]{1,2,0:T(8,128)(2,1)}), bf16[16,128,512]{1,2,0:T(8,128)(2,1)}, u32[]{:S(2)}, u32[]{:S(2)}) %all-to-all-start.2) | async-done | bytes 2097184 | tf_op jit(solution)/shard_map/all_to_all | solution.py:83
  204.0 3.4 copy.57
  214.0 274.6 %all-reduce.6.cloned.1.call-done = (f32[256,256]{0,1:T(8,128)}, f32[256,256]{0,1:T(8,128)}, f32[256,256]{0,1:T(8,128)}) async-done(((f32[256,256]{0,1:T(8,128)}, f32[256,256]{0,1:T(8,128)}, f32[256,256]{0,1:T(8,128)}), (f32[256,256]{0,1:T(8,128)}, f32[256,256]{0,1:T(8,128)}, f32[256,256]{0,1:T(8,128)})) %all-reduce.6.cloned.1.call-update) | async-done | bytes 786448 | tf_op jit(solution)/shard_map/psum | solution.py:109
  493.2 155.8 %all-reduce.4.cloned.1.call-done = f32[512,256]{1,0:T(8,128)} async-done(((f32[512,256]{1,0:T(8,128)}), f32[512,256]{1,0:T(8,128)}) %all-reduce.4.cloned.1.call-update) | async-done | bytes 524304 | tf_op jit(solution)/shard_map/psum | solution.py:105
  649.0 1.3 constant_dynamic-slice_fusion.1
  (144 shorter events, 57.5 us)
Async XLA Ops:
  7.2 10.5 %copy-start = (bf16[512,256]{1,0:T(8,128)(2,1)S(1)}, bf16[512,256]{1,0:T(8,128)(2,1)}, u32[]{:S(2)}) copy-start(bf16[512,256]{1,0:T(8,128)(2,1)} %param.11) | copy-start | bytes 786436
  8.6 15.3 %all-to-all-start = ((s32[16,1,1]{2,1,0:T(1,128)}), s32[16,1,1]{2,1,0:T(1,128)S(1)}, u32[]{:S(2)}, u32[]{:S(2)}) async-start(s32[16,1,1]{2,1,0:T(1,128)} %copy.46), calls=%async_computation | async-start | bytes 16384 | tf_op jit(solution)/shard_map/all_to_all | solution.py:48
  26.2 5.1 copy-start.6
  26.2 5.3 copy-start.2
  26.2 5.3 copy-start.4
  26.2 52.3 %all-to-all-start.1 = ((bf16[16,128,512]{2,1,0:T(8,128)(2,1)}), bf16[16,128,512]{2,1,0:T(8,128)(2,1)S(1)}, u32[]{:S(2)}, u32[]{:S(2)}) async-start(bf16[16,128,512]{2,1,0:T(8,128)(2,1)} %gather_fusion), calls=%async_computation.1 | async-start | bytes 4194304 | tf_op jit(solution)/shard_map/all_to_all | solution.py:57
  80.2 1.7 copy-start.1
  149.9 6.9 %copy-start.3 = (bf16[256,256]{1,0:T(8,128)(2,1)S(1)}, bf16[256,256]{1,0:T(8,128)(2,1)}, u32[]{:S(2)}) copy-start(bf16[256,256]{1,0:T(8,128)(2,1)} %param.10) | copy-start | bytes 393220
  149.9 54.2 %all-to-all-start.2 = ((bf16[16,128,512]{1,2,0:T(8,128)(2,1)}), bf16[16,128,512]{1,2,0:T(8,128)(2,1)}, u32[]{:S(2)}, u32[]{:S(2)}) async-start(bf16[16,128,512]{1,2,0:T(8,128)(2,1)} %pad_maximum_fusion), calls=%async_computation.2 | async-start | bytes 4194304 | tf_op jit(solution)/shard_map/all_to_all | solution.py:83
  156.8 331.9 %all-reduce.6.cloned.1.call-start = ((), (), s32[]{:S(2)}) async-start(), calls=%async_computation.4 | async-start | bytes 1572864 | tf_op jit(solution)/shard_map/psum | solution.py:109
  208.0 3.4 copy-start.8
  208.7 3.1 copy-start.9
  211.3 1.8 copy-start.5
  211.3 1.8 copy-start.7
  211.4 437.6 %all-reduce.4.cloned.1.call-start = ((), (), s32[]{:S(2)}) async-start(), calls=%async_computation.3 | async-start | bytes 1048576 | tf_op jit(solution)/shard_map/psum | solution.py:105
Sparse Core Ops, SparseCore 0:
  211.5 277.0 all-reduce.5
  492.0 156.9 all-reduce.3
where the time goes:
time: 659 us; the launch traced here: 657 us
  waiting for transfers between devices  529 us (80%)
  matrix products  48.8 us (7%)
  local copies, waits for them, and re-layouts  38.4 us (6%)
  starting transfers between devices  21.1 us (3%)
  between operations  14.3 us (2%)
    psum x1, waiting for transfers between devices, per_device(): weight_sums = lax.psum((wq_term, wk_term, wv_term), ('grp', 'ops'))  275 us
    psum x1, waiting for transfers between devices, per_device(): summed_total = lax.psum(machine_part, 'ops')  156 us
    all_to_all x1, waiting for transfers between devices, per_device(): lax.all_to_all(outgoing, 'grp', split_axis=0, concat_axis=0, tiled=True)  46.8 us
    all_to_all x1, waiting for transfers between devices, per_device(): lax.all_to_all(jnp.concatenate([key_grads, value_grads], axis=2), 'grp',...  46.3 us
    dot_general x16, matrix products, slot_grads(): jnp.einsum('ohc,mhc->ohm', cotangent4, value_rows, preferred_element_type...  20.9 us
  transfers between devices with their start and end apart: 5, of which 5 were waited for; matrix products, arithmetic and copies ran while one was open for 1% of the time, Pallas kernels for 0%

commit v1 on v0

--- a/solution.py
+++ b/solution.py
@@ -106,7 +106,7 @@
     share_rows = machine_rows // lax.axis_size("ops")
     first_row = lax.axis_index("ops") * share_rows
     machine_grad = lax.dynamic_slice_in_dim(summed_total, first_row, share_rows, 0)
-    weight_sums = lax.psum((wq_term, wk_term, wv_term), ("grp", "ops"))
+    weight_sums = lax.psum(lax.psum((wq_term, wk_term, wv_term), "ops"), "grp")
     shard_count = float(groups * lax.axis_size("ops"))
     grad_wq = weight_sums[0] / shard_count
     grad_wk = weight_sums[1] / shard_count

time: 659 us -> 523 us (0.79)
  the two profiles are of different devices: /device:TPU:8 before, /device:TPU:1 now
where the time goes in v1:
time: 523 us; the launch traced here: 521 us
  waiting for transfers between devices  380 us (73%)
  matrix products  62.4 us (12%)
  local copies, waits for them, and re-layouts  37.5 us (7%)
  starting transfers between devices  20 us (4%)
  between operations  14.2 us (3%)
  other arithmetic  5.53 us (1%)
    psum x1, waiting for transfers between devices, per_device(): summed_total = lax.psum(machine_part, 'ops')  159 us
    psum x1, waiting for transfers between devices, per_device(): weight_sums = lax.psum(lax.psum((wq_term, wk_term, wv_term), 'ops'), 'grp')  119 us
    all_to_all x1, waiting for transfers between devices, per_device(): lax.all_to_all(outgoing, 'grp', split_axis=0, concat_axis=0, tiled=True)  48.8 us
    all_to_all x1, waiting for transfers between devices, per_device(): lax.all_to_all(jnp.concatenate([key_grads, value_grads], axis=2), 'grp',...  48.2 us
    dot_general x16, matrix products, slot_grads(): jnp.einsum('ohc,mhc->ohm', queries, key_rows, preferred_element_type=jnp....  21.3 us
    dot_general x16, matrix products, slot_grads(): jnp.einsum('ohm,mhc->ohc', dscore, key_rows, preferred_element_type=jnp.f...  16.9 us
    dynamic_slice x16, local copies, waits for them, and re-layouts, per_device(): lax.scan(per_slot, start_q, (key_slots, value_slots, counts.T))  11.3 us
    dynamic_update_slice x16, local copies, waits for them, and re-layouts, per_device(): lax.scan(per_slot, start_q, (key_slots, value_slots, counts.T))  11 us
  transfers between devices with their start and end apart: 5, of which 5 were waited for; matrix products, arithmetic and copies ran while one was open for 1% of the time, Pallas kernels for 0%

profile of v1, /device:TPU:1, one launch (start us, length us, event | category | flops | bytes accessed | tf_op | source)
XLA Modules:
  0.0 520.6 jit_solution(15627018179011689782)
XLA Ops:
  7.2 1.4 copy.46
  8.6 10.1 %all-to-all-start = ((s32[16,1,1]{2,1,0:T(1,128)}), s32[16,1,1]{2,1,0:T(1,128)S(1)}, u32[]{:S(2)}, u32[]{:S(2)}) async-start(s32[16,1,1]{2,1,0:T(1,128)} %copy.46), calls=%async_computation | async-start | bytes 16384 | tf_op jit(solution)/shard_map/all_to_all | solution.py:48
  19.9 5.7 %all-to-all-done = s32[16,1,1]{2,1,0:T(1,128)S(1)} async-done(((s32[16,1,1]{2,1,0:T(1,128)}), s32[16,1,1]{2,1,0:T(1,128)S(1)}, u32[]{:S(2)}, u32[]{:S(2)}) %all-to-all-start) | async-done | bytes 96 | tf_op jit(solution)/shard_map/all_to_all | solution.py:48
  26.1 2.0 gather_fusion
  28.1 5.0 all-to-all-start.1
  33.4 48.8 %all-to-all-done.1 = bf16[16,128,512]{2,1,0:T(8,128)(2,1)} async-done(((bf16[16,128,512]{2,1,0:T(8,128)(2,1)}), bf16[16,128,512]{2,1,0:T(8,128)(2,1)}, u32[]{:S(2)}, u32[]{:S(2)}) %all-to-all-start.1) | async-done | bytes 2097184 | tf_op jit(solution)/shard_map/all_to_all | solution.py:57
  82.2 1.7 fusion.38
  83.9 1.3 copy.47
  85.9 77.1 %while.15 = (s32[]{:T(128)}, f32[256,8,32]{0,2,1:T(8,128)S(1)}, bf16[16,128,256]{1,2,0:T(8,128)(2,1)}, bf16[16,128,256]{1,2,0:T(8,128)(2,1)}, bf16[16,128,8,32]{...) while((s32[]{:T(128)}, f32[256,8,32]{0,2,1:T(8,128)S(1)}, ...), condition=%wide.region_1.2_spmd.clone, body=%wide.region_0.1_spmd.clone.sunk | while | flops 87785472 | bytes 6361235 | solution.py:74
  85.9 1.3 fusion.79
  90.7 1.3 fusion.79
  95.6 1.3 fusion.79
  100.4 1.3 fusion.79
  105.2 1.3 fusion.79
  110.0 1.3 fusion.79
  114.8 1.3 fusion.79
  119.7 1.3 fusion.79
  124.5 1.3 fusion.79
  129.3 1.3 fusion.79
  134.1 1.3 fusion.79
  138.9 1.3 fusion.79
  143.8 1.3 fusion.79
  148.6 1.3 fusion.79
  153.4 1.3 fusion.79
  158.2 1.3 fusion.79
  163.0 3.1 pad_maximum_fusion
  166.1 4.8 all-to-all-start.2
  171.9 48.2 %all-to-all-done.2 = bf16[16,128,512]{1,2,0:T(8,128)(2,1)} async-done(((bf16[16,128,512]{1,2,0:T(8,128)(2,1)}), bf16[16,128,512]{1,2,0:T(8,128)(2,1)}, u32[]{:S(2)}, u32[]{:S(2)}) %all-to-all-start.2) | async-done | bytes 2097184 | tf_op jit(solution)/shard_map/all_to_all | solution.py:83
  220.1 3.4 copy.57
  229.3 159.0 %all-reduce.5.cloned.1.call-done = (f32[512,256]{1,0:T(8,128)}, f32[256,256]{0,1:T(8,128)}, f32[256,256]{0,1:T(8,128)}, f32[256,256]{0,1:T(8,128)}) async-done(((f32[512,256]{1,0:T(8,128)}, f32[256,256]{0,1:T(8,128)}, f32[256,256]{0,1:T(8,128)}, f32[256,256]{0,1:T(8,128)}), (f32[512,256]{1,0:T(8,128)}, f32[256,256]{0,1:T(8,128)}, f32[256,256]{0,1:T(8,128)}, ...) | async-done | bytes 1310736 | tf_op jit(solution)/shard_map/psum | solution.py:105
  389.3 1.3 constant_dynamic-slice_fusion.1
  390.6 118.6 %all-reduce.7.cloned.1.call-done = (f32[256,256]{0,1:T(8,128)}, f32[256,256]{0,1:T(8,128)}, f32[256,256]{0,1:T(8,128)}) async-done(((f32[256,256]{0,1:T(8,128)}, f32[256,256]{0,1:T(8,128)}, f32[256,256]{0,1:T(8,128)}), (f32[256,256]{0,1:T(8,128)}, f32[256,256]{0,1:T(8,128)}, f32[256,256]{0,1:T(8,128)})) %all-reduce.7.cloned.1.call-update) | async-done | bytes 786448 | tf_op jit(solution)/shard_map/psum | solution.py:109
  (140 shorter events, 70.2 us)
Async XLA Ops:
  7.2 11.5 %copy-start = (bf16[512,256]{1,0:T(8,128)(2,1)S(1)}, bf16[512,256]{1,0:T(8,128)(2,1)}, u32[]{:S(2)}) copy-start(bf16[512,256]{1,0:T(8,128)(2,1)} %param.11) | copy-start | bytes 786436
  8.6 17.1 %all-to-all-start = ((s32[16,1,1]{2,1,0:T(1,128)}), s32[16,1,1]{2,1,0:T(1,128)S(1)}, u32[]{:S(2)}, u32[]{:S(2)}) async-start(s32[16,1,1]{2,1,0:T(1,128)} %copy.46), calls=%async_computation | async-start | bytes 16384 | tf_op jit(solution)/shard_map/all_to_all | solution.py:48
  28.1 5.0 copy-start.4
  28.1 5.1 copy-start.1
  28.1 5.1 copy-start.2
  28.1 54.2 %all-to-all-start.1 = ((bf16[16,128,512]{2,1,0:T(8,128)(2,1)}), bf16[16,128,512]{2,1,0:T(8,128)(2,1)}, u32[]{:S(2)}, u32[]{:S(2)}) async-start(bf16[16,128,512]{2,1,0:T(8,128)(2,1)} %gather_fusion), calls=%async_computation.1 | async-start | bytes 4194304 | tf_op jit(solution)/shard_map/all_to_all | solution.py:57
  166.1 54.0 %all-to-all-start.2 = ((bf16[16,128,512]{1,2,0:T(8,128)(2,1)}), bf16[16,128,512]{1,2,0:T(8,128)(2,1)}, u32[]{:S(2)}, u32[]{:S(2)}) async-start(bf16[16,128,512]{1,2,0:T(8,128)(2,1)} %pad_maximum_fusion), calls=%async_computation.2 | async-start | bytes 4194304 | tf_op jit(solution)/shard_map/all_to_all | solution.py:83
  171.0 217.4 %all-reduce.5.cloned.1.call-start = ((), (), s32[]{:S(2)}) async-start(), calls=%async_computation.3 | async-start | bytes 2621440 | tf_op jit(solution)/shard_map/psum | solution.py:105
  224.1 0.9 copy-start.6
  225.0 3.0 copy-start.7
  228.0 160.4 %copy-start.3 = (bf16[256,256]{1,0:T(8,128)(2,1)S(1)}, bf16[256,256]{1,0:T(8,128)(2,1)}, u32[]{:S(2)}) copy-start(bf16[256,256]{1,0:T(8,128)(2,1)} %param.13) | copy-start | bytes 393220
  228.0 160.4 %copy-start.5 = (bf16[256,256]{1,0:T(8,128)(2,1)S(1)}, bf16[256,256]{1,0:T(8,128)(2,1)}, u32[]{:S(2)}) copy-start(bf16[256,256]{1,0:T(8,128)(2,1)} %param.12) | copy-start | bytes 393220
  229.2 279.9 %all-reduce.7.cloned.1.call-start = ((), (), s32[]{:S(2)}) async-start(), calls=%async_computation.4 | async-start | bytes 1572864 | tf_op jit(solution)/shard_map/psum | solution.py:109
Sparse Core Ops, SparseCore 0:
  229.4 158.9 all-reduce.4
  390.8 118.2 all-reduce.6
